TPU v7x, 32 devices: a whole 2x2x4 slice. The times are simulated.
32 devices in a mesh: seq: 8 (over z, y), chan: 4 (over x, core).
Axes of the slice: x: 2, y: 2, z: 4, core: 2. Of those that a mesh axis runs over, the one named last changes fastest.
Arguments:
- value: bfloat16 [1024, 4096], P('seq', 'chan'), may hold values from -6 to 6
- gate: bfloat16 [1024, 4096], P('seq', 'chan'), may hold values from -6 to 6
- long_filter: bfloat16 [4096, 1024], P('chan', 'seq'), may hold values from -0.5 to 0.5
- skip_gain: float32 [4096], P('chan'), may hold values from 0.5 to 2
- cotangent: bfloat16 [1024, 4096], P('seq', 'chan'), may hold values from -6 to 6
- owner_map: int32 [8], replicated, may hold values from 0 to 7, each once
Outputs:
- output: bfloat16 [1024, 4096], P('seq', 'chan')
- value_grad: bfloat16 [1024, 4096], P('seq', 'chan')
- gate_grad: bfloat16 [1024, 4096], P('seq', 'chan')
- gain_grad: float32 [4, 8, 128], P('chan', 'seq')
Inputs may be any that keep to these rules, and one draw needn't show every extreme that they name: `owner_map`: a permutation: each index of seq once.
All inputs are finite; a program needn't handle non-finite values.
Results may differ from a plain program's by a relative error of at most 0.008.
Values may be sent and summed in bfloat16 or wider, within the bound.
A program may use at most 64 MiB of HBM per device.

v0:
```python
import functools
import math

import jax
import jax.numpy as jnp
import numpy as np
from jax import lax
from jax.experimental import pallas as pl
from jax.experimental.pallas import tpu as pltpu
from jax.sharding import PartitionSpec as P

HIGHEST = lax.Precision.HIGHEST


def dft_table(size):
    index = jnp.arange(size, dtype=jnp.int32)
    phase = index[:, None] * index[None, :] % size
    angle = 2.0 * math.pi / size * phase.astype(jnp.float32)
    return (jnp.cos(angle), jnp.sin(angle))


def make_tables(outer, inner):
    cos_outer, sin_outer = dft_table(outer)
    cos_inner, sin_inner = dft_table(inner)
    total = outer * inner
    phase = (
        jnp.arange(outer, dtype=jnp.int32)[:, None]
        * jnp.arange(inner, dtype=jnp.int32)[None, :]
        % total
    )
    angle = 2.0 * math.pi / total * phase.astype(jnp.float32)
    return (cos_outer, sin_outer, cos_inner, sin_inner, jnp.cos(angle), jnp.sin(angle))


def forward_dft(signal, tables):
    cos_outer, sin_outer, cos_inner, sin_inner, turn_cos, turn_sin = tables
    blocks = signal.shape[0]
    real_part = jnp.einsum("kn,ncb->ckb", cos_outer[:, :blocks], signal, precision=HIGHEST)
    imag_part = -jnp.einsum("kn,ncb->ckb", sin_outer[:, :blocks], signal, precision=HIGHEST)
    twisted_real = real_part * turn_cos + imag_part * turn_sin
    twisted_imag = imag_part * turn_cos - real_part * turn_sin
    spec_real = jnp.einsum("ckn,nm->ckm", twisted_real, cos_inner, precision=HIGHEST) + jnp.einsum(
        "ckn,nm->ckm", twisted_imag, sin_inner, precision=HIGHEST
    )
    spec_imag = jnp.einsum("ckn,nm->ckm", twisted_imag, cos_inner, precision=HIGHEST) - jnp.einsum(
        "ckn,nm->ckm", twisted_real, sin_inner, precision=HIGHEST
    )
    return (spec_real, spec_imag)


def inverse_dft(spec_real, spec_imag, tables, blocks):
    cos_outer, sin_outer, cos_inner, sin_inner, turn_cos, turn_sin = tables
    total = cos_outer.shape[0] * cos_inner.shape[0]
    inner_real = jnp.einsum("ckm,mn->ckn", spec_real, cos_inner, precision=HIGHEST) - jnp.einsum(
        "ckm,mn->ckn", spec_imag, sin_inner, precision=HIGHEST
    )
    inner_imag = jnp.einsum("ckm,mn->ckn", spec_real, sin_inner, precision=HIGHEST) + jnp.einsum(
        "ckm,mn->ckn", spec_imag, cos_inner, precision=HIGHEST
    )
    turned_real = inner_real * turn_cos - inner_imag * turn_sin
    turned_imag = inner_real * turn_sin + inner_imag * turn_cos
    result = jnp.einsum(
        "nk,ckb->ncb", cos_outer[:blocks, :], turned_real, precision=HIGHEST
    ) - jnp.einsum("nk,ckb->ncb", sin_outer[:blocks, :], turned_imag, precision=HIGHEST)
    return result / total


def causal_conv(sent_value, filter_spec, tables):
    value_real, value_imag = forward_dft(sent_value.astype(jnp.float32), tables)
    filter_real, filter_imag = filter_spec
    product_real = value_real * filter_real - value_imag * filter_imag
    product_imag = value_real * filter_imag + value_imag * filter_real
    return inverse_dft(product_real, product_imag, tables, sent_value.shape[0]).astype(jnp.bfloat16)


def transposed_conv(sent_grad, filter_spec, tables):
    grad_real, grad_imag = forward_dft(sent_grad.astype(jnp.float32), tables)
    filter_real, filter_imag = filter_spec
    product_real = grad_real * filter_real + grad_imag * filter_imag
    product_imag = grad_imag * filter_real - grad_real * filter_imag
    return inverse_dft(product_real, product_imag, tables, sent_grad.shape[0]).astype(jnp.bfloat16)


def split_body(value, gate, long_filter, skip_gain, cotangent, owner_map):
    blocks = lax.axis_size("seq")
    tok_rows = value.shape[0]
    group = value.shape[1]
    per_device = group // blocks
    value_rows = value.astype(jnp.float32)
    gate_rows = gate.astype(jnp.float32)
    grad_rows = (cotangent.astype(jnp.float32) * gate_rows).astype(jnp.bfloat16)
    value_major = value.T
    grad_major = grad_rows.T
    tables = make_tables(2 * blocks, tok_rows)
    value_split = value_major.reshape(blocks, per_device, tok_rows)
    filter_split = long_filter.reshape(blocks, per_device, tok_rows)
    grad_split = grad_major.reshape(blocks, per_device, tok_rows)
    sent_value, sent_filter = (
        lax.all_to_all(value_split, "seq", split_axis=0, concat_axis=0, tiled=True),
        lax.all_to_all(filter_split, "seq", split_axis=0, concat_axis=0, tiled=True),
    )
    filter_spec = forward_dft(sent_filter.astype(jnp.float32), tables)
    conv_back = lax.all_to_all(
        causal_conv(sent_value, filter_spec, tables), "seq", split_axis=0, concat_axis=0, tiled=True
    )
    sent_grad = lax.all_to_all(grad_split, "seq", split_axis=0, concat_axis=0, tiled=True)
    grad_back = lax.all_to_all(
        transposed_conv(sent_grad, filter_spec, tables),
        "seq",
        split_axis=0,
        concat_axis=0,
        tiled=True,
    )
    conv_rows = conv_back.reshape(group, tok_rows).T.astype(jnp.float32)
    mixed = conv_rows + skip_gain * value_rows
    output = (gate_rows * mixed).astype(jnp.bfloat16)
    gate_grad = (cotangent.astype(jnp.float32) * mixed).astype(jnp.bfloat16)
    back_rows = grad_back.reshape(group, tok_rows).T.astype(jnp.float32)
    grad_float = grad_rows.astype(jnp.float32)
    value_grad = (back_rows + skip_gain * grad_float).astype(jnp.bfloat16)
    scale = 1.0 / math.sqrt(tok_rows * blocks)
    local_sums = (
        jnp.sum(sent_value.astype(jnp.float32) * sent_grad.astype(jnp.float32), axis=(0, 2)) * scale
    )
    gathered = lax.all_gather(local_sums.reshape(1, per_device), "seq", axis=0, tiled=True)
    mine = owner_map[lax.axis_index("seq")]
    summed = lax.dynamic_slice_in_dim(gathered, mine, 1, 0)
    gain_grad = summed.reshape(1, 1, per_device)
    return (output, value_grad, gate_grad, gain_grad)


LANES = 128
FILTER, VALUE, GRAD, CONV, BACK, SUMS = range(6)
MESH = pl.DeviceIdType.MESH


def base_tables(length):
    unit = 2.0 * math.pi / (16 * length)
    row = 4 * np.arange(length, dtype=np.int64)[:, None] + 1
    lane = 4 * np.arange(LANES, dtype=np.int64)[None, :] + 1
    angle = unit * (row * lane % (16 * length))
    block = 4 * LANES * np.arange(length // LANES, dtype=np.int64)[None, :]
    step = unit * (row * block % (16 * length))
    quarter = unit * row
    turn = np.concatenate([np.cos(step), np.sin(step), np.cos(quarter), np.sin(quarter)], axis=1)
    turn = np.pad(turn, ((0, 0), (0, -turn.shape[1] % LANES)))
    return tuple(t.astype(np.float32) for t in (np.cos(angle), np.sin(angle), turn))


def split(wide):
    high = wide.astype(jnp.bfloat16)
    return high, (wide - high.astype(jnp.float32)).astype(jnp.bfloat16)


def fused_kernel(
    n,
    value,
    filt,
    gate,
    cot,
    skip,
    owner,
    base_cos,
    base_sin,
    turn,
    out,
    value_grad,
    gate_grad,
    gain,
    value_loc,
    gate_loc,
    cot_loc,
    grad_loc,
    cos_hi,
    cos_lo,
    sin_hi,
    sin_lo,
    seq_value,
    seq_filter,
    taps,
    seq_grad,
    spec_c,
    spec_d,
    spec_a,
    spec_b,
    prod_cos,
    prod_sin,
    conv_out,
    back_out,
    conv_in,
    back_in,
    sums_out,
    sums_in,
    send_sem,
    recv_sem,
    local_sem,
):
    me = lax.axis_index("seq")
    rows, group = value.shape
    chans = group // n
    length = rows * n
    half = length // 2
    offsets = sorted(range(1, n), key=lambda i: abs(2 * i - n))
    blocks = length // LANES

    def peer_of(offset):
        return lax.rem(me + offset, n)

    def cols(index):
        return pl.ds(pl.multiple_of(index * chans, chans), chans)

    def seq_rows(index):
        return pl.ds(pl.multiple_of(index * rows, rows), rows)

    def transfer(kind, source, target, peer, sender):
        return pltpu.make_async_remote_copy(
            src_ref=source,
            dst_ref=target,
            send_sem=send_sem.at[kind, peer],
            recv_sem=recv_sem.at[kind, sender],
            device_id={"seq": peer},
            device_id_type=MESH,
        )

    def copy_of(kind, peer, sender):
        if kind == FILTER:
            pair = filt.at[cols(peer), :], seq_filter.at[sender]
        elif kind == VALUE:
            pair = value.at[:, cols(peer)], seq_value.at[seq_rows(sender), :]
        elif kind == GRAD:
            pair = grad_loc.at[:, cols(peer)], seq_grad.at[seq_rows(sender), :]
        elif kind == CONV:
            pair = conv_out.at[seq_rows(peer), :], conv_in.at[sender]
        elif kind == BACK:
            pair = back_out.at[seq_rows(peer), :], back_in.at[sender]
        else:
            pair = sums_out, sums_in.at[sender]
        return transfer(kind, *pair, peer, sender)

    def send(kind, peer):
        copy_of(kind, peer, me).start()

    def receive(kind):
        for offset in reversed(offsets):
            peer = peer_of(offset)
            copy_of(kind, peer, peer).wait_recv()

    barrier = pltpu.get_barrier_semaphore()
    for offset in offsets:
        pl.semaphore_signal(barrier, inc=1, device_id={"seq": peer_of(offset)}, device_id_type=MESH)
    local = [
        pltpu.make_async_copy(gate, gate_loc, local_sem.at[0]),
        pltpu.make_async_copy(cot, cot_loc, local_sem.at[1]),
        pltpu.make_async_copy(value, value_loc, local_sem.at[2]),
        pltpu.make_async_copy(filt.at[cols(me), :], seq_filter.at[me], local_sem.at[3]),
        pltpu.make_async_copy(value.at[:, cols(me)], seq_value.at[seq_rows(me), :], local_sem.at[4]),
    ]
    for copy in local:
        copy.start()
    pl.semaphore_wait(barrier, n - 1)
    for kind in (FILTER, VALUE):
        for offset in offsets:
            send(kind, peer_of(offset))

    local[0].wait()
    local[1].wait()
    grad_loc[...] = (cot_loc[...].astype(jnp.float32) * gate_loc[...].astype(jnp.float32)).astype(
        jnp.bfloat16
    )
    seq_grad[seq_rows(me), :] = grad_loc[:, cols(me)]
    for offset in offsets:
        send(GRAD, peer_of(offset))

    @pl.loop(0, length // LANES)
    def _(step):
        at = pl.ds(pl.multiple_of(step * LANES, LANES), LANES)
        lane_cos, lane_sin = base_cos[at, :], base_sin[at, :]
        for block in range(blocks):
            block_cos = turn[at, block : block + 1]
            block_sin = turn[at, blocks + block : blocks + block + 1]
            to = pl.ds(block * LANES, LANES)
            cos_hi[at, to], cos_lo[at, to] = split(lane_cos * block_cos - lane_sin * block_sin)
            sin_hi[at, to], sin_lo[at, to] = split(lane_sin * block_cos + lane_cos * block_sin)

    def forward(signal, real, imag):
        @pl.loop(0, 2)
        def _(step):
            at = pl.ds(pl.multiple_of(step * half, half), half)
            for high, low, spec in ((cos_hi, cos_lo, real), (sin_hi, sin_lo, imag)):
                spec[at, :] = jnp.dot(
                    high[at, :], signal[...], preferred_element_type=jnp.float32
                ) + jnp.dot(low[at, :], signal[...], preferred_element_type=jnp.float32)

    def put_product(on_cos, on_sin):
        for wide, store in ((on_cos, prod_cos), (on_sin, prod_sin)):
            high, low = split(wide)
            store[:, :chans] = high
            store[:, chans:] = low

    def inverse(result, kind):
        mine = me // (n // 2)

        @pl.loop(0, 2)
        def _(step):
            part = lax.rem(mine + 1 + step, 2)
            at = pl.ds(pl.multiple_of(part * half, half), half)
            both = jnp.dot(
                cos_hi[at, :], prod_cos[...], preferred_element_type=jnp.float32
            ) + jnp.dot(sin_hi[at, :], prod_sin[...], preferred_element_type=jnp.float32)
            low = jnp.dot(
                cos_lo[at, :], prod_cos[:, :chans], preferred_element_type=jnp.float32
            ) + jnp.dot(sin_lo[at, :], prod_sin[:, :chans], preferred_element_type=jnp.float32)
            result[at, :] = (both[:, :chans] + (both[:, chans:] + low)).astype(jnp.bfloat16)
            for index in range(n // 2):
                to = part * (n // 2) + lax.rem(me + index, n // 2)

                @pl.when(to != me)
                def _():
                    send(kind, to)

    local[3].wait()
    receive(FILTER)
    for index in range(n):
        taps[index * rows : (index + 1) * rows, :] = (
            seq_filter[index].astype(jnp.float32).T.astype(jnp.bfloat16)
        )
    forward(taps, spec_a, spec_b)
    quarter_cos = turn[:, 2 * blocks : 2 * blocks + 1] * (1.0 / length)
    quarter_sin = turn[:, 2 * blocks + 1 : 2 * blocks + 2] * (1.0 / length)
    spec_c[...] = spec_a[...] * quarter_cos + spec_b[...] * quarter_sin
    spec_d[...] = spec_b[...] * quarter_cos - spec_a[...] * quarter_sin

    local[4].wait()
    receive(VALUE)
    forward(seq_value, spec_a, spec_b)
    put_product(
        spec_a[...] * spec_c[...] - spec_b[...] * spec_d[...],
        spec_a[...] * spec_d[...] + spec_b[...] * spec_c[...],
    )
    inverse(conv_out, CONV)

    receive(GRAD)
    forward(seq_grad, spec_a, spec_b)
    put_product(
        spec_a[...] * spec_c[...] + spec_b[...] * spec_d[...],
        spec_b[...] * spec_c[...] - spec_a[...] * spec_d[...],
    )
    inverse(back_out, BACK)
    sums = jnp.sum(
        seq_value[...].astype(jnp.float32) * seq_grad[...].astype(jnp.float32), axis=0, keepdims=True
    ) * (1.0 / math.sqrt(length))
    sums_out[...] = jnp.broadcast_to(sums, sums_out.shape)
    sums_in[me] = jnp.broadcast_to(sums, sums_out.shape)
    for offset in offsets:
        send(SUMS, peer_of(offset))

    local[2].wait()

    def finish_conv(index, conv):
        at = cols(index)
        mixed = conv.astype(jnp.float32) + skip[:, at] * value_loc[:, at].astype(jnp.float32)
        out[:, at] = (gate_loc[:, at].astype(jnp.float32) * mixed).astype(jnp.bfloat16)
        gate_grad[:, at] = (cot_loc[:, at].astype(jnp.float32) * mixed).astype(jnp.bfloat16)

    def finish_back(index, back):
        at = cols(index)
        value_grad[:, at] = (
            back.astype(jnp.float32) + skip[:, at] * grad_loc[:, at].astype(jnp.float32)
        ).astype(jnp.bfloat16)

    finish_conv(me, conv_out[seq_rows(me), :])
    finish_back(me, back_out[seq_rows(me), :])
    for kind, finish, landed in ((CONV, finish_conv, conv_in), (BACK, finish_back, back_in)):
        for offset in reversed(offsets):
            peer = peer_of(offset)
            copy_of(kind, peer, peer).wait_recv()
            finish(peer, landed[peer])
    receive(SUMS)
    gain[...] = sums_in[owner[me]][:1, :]
    for kind in range(6):
        for offset in offsets:
            peer = peer_of(offset)
            copy_of(kind, peer, me).wait_send()


def fused_body(value, gate, long_filter, skip_gain, cotangent, owner_map):
    n = lax.axis_size("seq")
    rows, group = value.shape
    chans = group // n
    length = rows * n
    base_cos, base_sin, turn = base_tables(length)
    anywhere = pl.BlockSpec(memory_space=pl.ANY)
    vmem = pl.BlockSpec(memory_space=pltpu.VMEM)
    bf16, f32 = jnp.bfloat16, jnp.float32
    table = pltpu.VMEM((length, length), bf16)
    spec = pltpu.VMEM((length, chans), f32)
    tokens = pltpu.VMEM((rows, group), bf16)
    sequence = pltpu.VMEM((length, chans), bf16)
    landing = pltpu.VMEM((n, rows, chans), bf16)
    output, value_grad, gate_grad, gain = pl.pallas_call(
        functools.partial(fused_kernel, n),
        out_shape=(
            jax.ShapeDtypeStruct((rows, group), bf16),
            jax.ShapeDtypeStruct((rows, group), bf16),
            jax.ShapeDtypeStruct((rows, group), bf16),
            jax.ShapeDtypeStruct((1, chans), f32),
        ),
        in_specs=[
            anywhere,
            anywhere,
            anywhere,
            anywhere,
            vmem,
            pl.BlockSpec(memory_space=pltpu.SMEM),
            vmem,
            vmem,
            vmem,
        ],
        out_specs=(vmem, vmem, vmem, vmem),
        scratch_shapes=[
            tokens,
            tokens,
            tokens,
            tokens,
            table,
            table,
            table,
            table,
            sequence,
            pltpu.VMEM((n, chans, rows), bf16),
            sequence,
            sequence,
            spec,
            spec,
            spec,
            spec,
            pltpu.VMEM((length, 2 * chans), bf16),
            pltpu.VMEM((length, 2 * chans), bf16),
            sequence,
            sequence,
            landing,
            landing,
            pltpu.VMEM((8, chans), f32),
            pltpu.VMEM((n, 8, chans), f32),
            pltpu.SemaphoreType.DMA((6, n)),
            pltpu.SemaphoreType.DMA((6, n)),
            pltpu.SemaphoreType.DMA((5,)),
        ],
        compiler_params=pltpu.CompilerParams(collective_id=0, has_side_effects=True),
    )(
        value,
        long_filter,
        gate,
        cotangent,
        skip_gain.reshape(1, group),
        owner_map,
        base_cos,
        base_sin,
        turn,
    )
    return (output, value_grad, gate_grad, gain.reshape(1, 1, chans))


def body(value, gate, long_filter, skip_gain, cotangent, owner_map):
    n = lax.axis_size("seq")
    rows, group = value.shape
    aligned = rows % LANES == 0 and group % (n * LANES) == 0 and n % 2 == 0
    tables_fit = 8 * (rows * n) ** 2 <= 16 * 2**20
    chosen = fused_body if aligned and tables_fit else split_body
    return chosen(value, gate, long_filter, skip_gain, cotangent, owner_map)


def solution(mesh):
    in_specs = (
        P("seq", "chan"),
        P("seq", "chan"),
        P("chan", "seq"),
        P("chan"),
        P("seq", "chan"),
        P(),
    )
    out_specs = (P("seq", "chan"), P("seq", "chan"), P("seq", "chan"), P("chan", "seq", None))
    return jax.shard_map(body, mesh=mesh, in_specs=in_specs, out_specs=out_specs, check_vma=False)
```

profile of v0, /device:TPU:0, one launch (start us, length us, event | category | flops | bytes accessed | tf_op | source)
XLA Modules:
  0.0 46.1 jit_solution(3606827429290657780)
XLA Ops:
  0.6 41.5 %shard_map.120 = (bf16[128,1024]{1,0:T(8,128)(2,1)}, bf16[128,1024]{1,0:T(8,128)(2,1)}, bf16[128,1024]{1,0:T(8,128)(2,1)}, f32[1,128]{1,0:T(1,128)}) custom-call(bf16[128,1024]{1,0:T(8,128)(2,1)} %value.1, bf16[1024,128]{1,0:T(8,128)(2,1)} %filt.1, bf16[128,1024]{1,0:T(8,128)(2,1)} %gate.1, bf16[128,1024]{1,0:T(8,128)(2,1)} %cot.1, f32[1,1024]{1,0:T(1,128)} %bitcast.2, ...), custom_call_target="tpu_custom_call" | custom-call | tf_op jit(solution)/shard_map/pallas_call | solution.py:400
  42.1 0.0 copy-start.1
  42.1 1.7 %copy.17 = bf16[128,1024]{1,0:T(8,128)(2,1)} copy(bf16[128,1024]{1,0:T(8,128)(2,1)} %get-tuple-element.16) | data formatting | bytes 524288
  43.8 0.0 copy-done.1
  43.8 0.0 copy-start
  43.8 0.7 %copy.18 = bf16[128,1024]{1,0:T(8,128)(2,1)} copy(bf16[128,1024]{1,0:T(8,128)(2,1)S(1)} %copy-done.1) | data formatting | bytes 524288
  44.5 0.3 copy-done
  44.9 0.0 copy-start.2
  44.9 0.7 %copy.19 = bf16[128,1024]{1,0:T(8,128)(2,1)} copy(bf16[128,1024]{1,0:T(8,128)(2,1)S(1)} %copy-done) | data formatting | bytes 524288
  45.6 0.0 copy-done.2
  45.6 0.5 %copy.20 = f32[1,1,128]{2,1,0:T(1,128)} copy(f32[1,1,128]{2,1,0:T(1,128)S(1)} %bitcast.3) | data formatting | bytes 1024
Async XLA Ops:
  42.1 1.7 %copy-start.1 = (bf16[128,1024]{1,0:T(8,128)(2,1)S(1)}, bf16[128,1024]{1,0:T(8,128)(2,1)}, u32[]{:S(2)}) copy-start(bf16[128,1024]{1,0:T(8,128)(2,1)} %get-tuple-element.17) | copy-start | bytes 786436
  43.8 1.0 %copy-start = (bf16[128,1024]{1,0:T(8,128)(2,1)S(1)}, bf16[128,1024]{1,0:T(8,128)(2,1)}, u32[]{:S(2)}) copy-start(bf16[128,1024]{1,0:T(8,128)(2,1)} %get-tuple-element.18) | copy-start | bytes 786436
  44.9 0.7 %copy-start.2 = (f32[1,128]{1,0:T(1,128)S(1)}, f32[1,128]{1,0:T(1,128)}, u32[]{:S(2)}) copy-start(f32[1,128]{1,0:T(1,128)} %get-tuple-element.11) | copy-start | bytes 1540
where the time goes:
time: 46.3 us; the launch traced here: 46.1 us
  Pallas kernels  41.5 us (90%)
  local copies, waits for them, and re-layouts  3.98 us (9%)
  between operations  0.65 us (1%)
    pallas_call x1, Pallas kernels, fused_body(): pl.pallas_call(functools.partial(fused_kernel, n), out_shape=(jax.ShapeDt...  41.5 us
    unnamed x10, local copies, waits for them, and re-layouts  3.98 us

commit v1 on v0

--- a/solution.py
+++ b/solution.py
@@ -160,13 +160,15 @@
     cot,
     skip,
     owner,
+    base_cos_any,
+    base_sin_any,
+    turn_any,
+    out,
+    value_grad,
+    gain,
     base_cos,
     base_sin,
     turn,
-    out,
-    value_grad,
-    gate_grad,
-    gain,
     value_loc,
     gate_loc,
     cot_loc,
@@ -254,6 +256,9 @@
         pltpu.make_async_copy(value, value_loc, local_sem.at[2]),
         pltpu.make_async_copy(filt.at[cols(me), :], seq_filter.at[me], local_sem.at[3]),
         pltpu.make_async_copy(value.at[:, cols(me)], seq_value.at[seq_rows(me), :], local_sem.at[4]),
+        pltpu.make_async_copy(base_cos_any, base_cos, local_sem.at[5]),
+        pltpu.make_async_copy(base_sin_any, base_sin, local_sem.at[6]),
+        pltpu.make_async_copy(turn_any, turn, local_sem.at[7]),
     ]
     for copy in local:
         copy.start()
@@ -270,6 +275,9 @@
     seq_grad[seq_rows(me), :] = grad_loc[:, cols(me)]
     for offset in offsets:
         send(GRAD, peer_of(offset))
+
+    for copy in local[5:]:
+        copy.wait()
 
     @pl.loop(0, length // LANES)
     def _(step):
@@ -340,12 +348,6 @@
     inverse(conv_out, CONV)
 
     receive(GRAD)
-    forward(seq_grad, spec_a, spec_b)
-    put_product(
-        spec_a[...] * spec_c[...] + spec_b[...] * spec_d[...],
-        spec_b[...] * spec_c[...] - spec_a[...] * spec_d[...],
-    )
-    inverse(back_out, BACK)
     sums = jnp.sum(
         seq_value[...].astype(jnp.float32) * seq_grad[...].astype(jnp.float32), axis=0, keepdims=True
     ) * (1.0 / math.sqrt(length))
@@ -354,19 +356,19 @@
     for offset in offsets:
         send(SUMS, peer_of(offset))
 
+    forward(seq_grad, spec_a, spec_b)
+    put_product(
+        spec_a[...] * spec_c[...] + spec_b[...] * spec_d[...],
+        spec_b[...] * spec_c[...] - spec_a[...] * spec_d[...],
+    )
+    inverse(back_out, BACK)
     local[2].wait()
 
     def finish_conv(index, conv):
-        at = cols(index)
-        mixed = conv.astype(jnp.float32) + skip[:, at] * value_loc[:, at].astype(jnp.float32)
-        out[:, at] = (gate_loc[:, at].astype(jnp.float32) * mixed).astype(jnp.bfloat16)
-        gate_grad[:, at] = (cot_loc[:, at].astype(jnp.float32) * mixed).astype(jnp.bfloat16)
+        out[:, cols(index)] = conv
 
     def finish_back(index, back):
-        at = cols(index)
-        value_grad[:, at] = (
-            back.astype(jnp.float32) + skip[:, at] * grad_loc[:, at].astype(jnp.float32)
-        ).astype(jnp.bfloat16)
+        value_grad[:, cols(index)] = back
 
     finish_conv(me, conv_out[seq_rows(me), :])
     finish_back(me, back_out[seq_rows(me), :])
@@ -383,13 +385,25 @@
             copy_of(kind, peer, me).wait_send()
 
 
+def finish_kernel(
+    conv, back, value, gate, cot, skip, gathered, output, value_grad, gate_grad, gain
+):
+    gate_rows, cot_rows = gate[...].astype(jnp.float32), cot[...].astype(jnp.float32)
+    grads = (cot_rows * gate_rows).astype(jnp.bfloat16).astype(jnp.float32)
+    mixed = conv[...].astype(jnp.float32) + skip[...] * value[...].astype(jnp.float32)
+    output[...] = (gate_rows * mixed).astype(jnp.bfloat16)
+    gate_grad[...] = (cot_rows * mixed).astype(jnp.bfloat16)
+    value_grad[...] = (back[...].astype(jnp.float32) + skip[...] * grads).astype(jnp.bfloat16)
+    gain[...] = gathered[...]
+
+
 def fused_body(value, gate, long_filter, skip_gain, cotangent, owner_map):
     n = lax.axis_size("seq")
     rows, group = value.shape
     chans = group // n
     length = rows * n
     base_cos, base_sin, turn = base_tables(length)
-    anywhere = pl.BlockSpec(memory_space=pl.ANY)
+    anywhere = pl.BlockSpec(memory_space=pltpu.HBM)
     vmem = pl.BlockSpec(memory_space=pltpu.VMEM)
     bf16, f32 = jnp.bfloat16, jnp.float32
     table = pltpu.VMEM((length, length), bf16)
@@ -397,10 +411,9 @@
     tokens = pltpu.VMEM((rows, group), bf16)
     sequence = pltpu.VMEM((length, chans), bf16)
     landing = pltpu.VMEM((n, rows, chans), bf16)
-    output, value_grad, gate_grad, gain = pl.pallas_call(
+    conv, back, gain = pl.pallas_call(
         functools.partial(fused_kernel, n),
         out_shape=(
-            jax.ShapeDtypeStruct((rows, group), bf16),
             jax.ShapeDtypeStruct((rows, group), bf16),
             jax.ShapeDtypeStruct((rows, group), bf16),
             jax.ShapeDtypeStruct((1, chans), f32),
@@ -412,12 +425,15 @@
             anywhere,
             vmem,
             pl.BlockSpec(memory_space=pltpu.SMEM),
-            vmem,
-            vmem,
-            vmem,
+            anywhere,
+            anywhere,
+            anywhere,
         ],
-        out_specs=(vmem, vmem, vmem, vmem),
+        out_specs=(vmem, vmem, vmem),
         scratch_shapes=[
+            pltpu.VMEM(base_cos.shape, f32),
+            pltpu.VMEM(base_sin.shape, f32),
+            pltpu.VMEM(turn.shape, f32),
             tokens,
             tokens,
             tokens,
@@ -444,9 +460,11 @@
             pltpu.VMEM((n, 8, chans), f32),
             pltpu.SemaphoreType.DMA((6, n)),
             pltpu.SemaphoreType.DMA((6, n)),
-            pltpu.SemaphoreType.DMA((5,)),
+            pltpu.SemaphoreType.DMA((8,)),
         ],
-        compiler_params=pltpu.CompilerParams(collective_id=0, has_side_effects=True),
+        compiler_params=pltpu.CompilerParams(
+            collective_id=0, has_side_effects=True
+        ),
     )(
         value,
         long_filter,
@@ -458,6 +476,20 @@
         base_sin,
         turn,
     )
+    output, value_grad, gate_grad, gain = pl.pallas_call(
+        finish_kernel,
+        grid=(2,),
+        out_shape=(
+            jax.ShapeDtypeStruct((rows, group), bf16),
+            jax.ShapeDtypeStruct((rows, group), bf16),
+            jax.ShapeDtypeStruct((rows, group), bf16),
+            jax.ShapeDtypeStruct((1, chans), f32),
+        ),
+        in_specs=[pl.BlockSpec((rows // 2, group), lambda i: (i, 0))] * 5
+        + [pl.BlockSpec((1, group), lambda i: (0, 0)), pl.BlockSpec((1, chans), lambda i: (0, 0))],
+        out_specs=[pl.BlockSpec((rows // 2, group), lambda i: (i, 0))] * 3
+        + [pl.BlockSpec((1, chans), lambda i: (0, 0))],
+    )(conv, back, value, gate, cotangent, skip_gain.reshape(1, group), gain)
     return (output, value_grad, gate_grad, gain.reshape(1, 1, chans))
 
 

time: 46.3 us -> 43.4 us (0.937)
  local copies, waits for them, and re-layouts: 3.98 us -> 0 us
  Pallas kernels: 41.5 us -> 42.5 us
    unnamed x10 -> x0, local copies, waits for them, and re-layouts: 3.98 us -> none
    pallas_call x0 -> x1, Pallas kernels: none -> 2.24 us  [fused_body(): pl.pallas_call(finish_kernel, grid=(2,), out_shape=(jax.ShapeDtypeStruct(...]
    pallas_call x1, Pallas kernels: 41.5 us -> 40.3 us  [fused_body(): pl.pallas_call(functools.partial(fused_kernel, n), out_shape=(jax.ShapeDt...]
where the time goes in v1:
time: 43.4 us; the launch traced here: 43.2 us
  Pallas kernels  42.5 us (98%)
  between operations  0.64 us (1%)
    pallas_call x1, Pallas kernels, fused_body(): pl.pallas_call(functools.partial(fused_kernel, n), out_shape=(jax.ShapeDt...  40.3 us
    pallas_call x1, Pallas kernels, fused_body(): pl.pallas_call(finish_kernel, grid=(2,), out_shape=(jax.ShapeDtypeStruct(...  2.24 us

profile of v1, /device:TPU:0, one launch (start us, length us, event | category | flops | bytes accessed | tf_op | source)
XLA Modules:
  0.0 43.2 jit_solution(970632612496774146)
XLA Ops:
  0.6 40.3 %shard_map.120 = (bf16[128,1024]{1,0:T(8,128)(2,1)}, bf16[128,1024]{1,0:T(8,128)(2,1)}, f32[1,128]{1,0:T(1,128)}) custom-call(bf16[128,1024]{1,0:T(8,128)(2,1)} %value.3, bf16[1024,128]{1,0:T(8,128)(2,1)} %filt.1, bf16[128,1024]{1,0:T(8,128)(2,1)} %gate.3, bf16[128,1024]{1,0:T(8,128)(2,1)} %cot.3, f32[1,1024]{1,0:T(1,128)} %bitcast.2, s32[8]{0:T(128)} %owner.1, ...), custom_call_target="tpu_custom_call" | custom-call | tf_op jit(solution)/shard_map/pallas_call | solution.py:414
  40.9 2.2 %shard_map.121 = (bf16[128,1024]{1,0:T(8,128)(2,1)}, bf16[128,1024]{1,0:T(8,128)(2,1)}, bf16[128,1024]{1,0:T(8,128)(2,1)}, f32[1,128]{1,0:T(1,128)}) custom-call(bf16[128,1024]{1,0:T(8,128)(2,1)} %get-tuple-element.11.conv, bf16[128,1024]{1,0:T(8,128)(2,1)} %get-tuple-element.12.back, bf16[128,1024]{1,0:T(8,128)(2,1)} %value.3, bf16[128,1024]{1,0:T(8,128)(2,1)} %gate.3, ...), custom_call_target="tpu_custom_call" | custom-call | tf_op jit(solution)/shard_map/pallas_call | solution.py:479

commit v2 on v1

--- a/solution.py
+++ b/solution.py
@@ -291,13 +291,10 @@
             sin_hi[at, to], sin_lo[at, to] = split(lane_sin * block_cos + lane_cos * block_sin)
 
     def forward(signal, real, imag):
-        @pl.loop(0, 2)
-        def _(step):
-            at = pl.ds(pl.multiple_of(step * half, half), half)
-            for high, low, spec in ((cos_hi, cos_lo, real), (sin_hi, sin_lo, imag)):
-                spec[at, :] = jnp.dot(
-                    high[at, :], signal[...], preferred_element_type=jnp.float32
-                ) + jnp.dot(low[at, :], signal[...], preferred_element_type=jnp.float32)
+        for high, low, spec in ((cos_hi, cos_lo, real), (sin_hi, sin_lo, imag)):
+            spec[...] = jnp.dot(
+                high[...], signal[...], preferred_element_type=jnp.float32
+            ) + jnp.dot(low[...], signal[...], preferred_element_type=jnp.float32)
 
     def put_product(on_cos, on_sin):
         for wide, store in ((on_cos, prod_cos), (on_sin, prod_sin)):

time: 43.4 us -> 42.9 us (0.988)
    pallas_call x1, Pallas kernels: 40.3 us -> 39.8 us  [fused_body(): pl.pallas_call(functools.partial(fused_kernel, n), out_shape=(jax.ShapeDt...]
where the time goes in v2:
time: 42.9 us; the launch traced here: 42.7 us
  Pallas kernels  42.1 us (98%)
  between operations  0.64 us (1%)
    pallas_call x1, Pallas kernels, fused_body(): pl.pallas_call(functools.partial(fused_kernel, n), out_shape=(jax.ShapeDt...  39.8 us
    pallas_call x1, Pallas kernels, fused_body(): pl.pallas_call(finish_kernel, grid=(2,), out_shape=(jax.ShapeDtypeStruct(...  2.24 us

profile of v2, /device:TPU:0, one launch (start us, length us, event | category | flops | bytes accessed | tf_op | source)
XLA Modules:
  0.0 42.7 jit_solution(14203760475687009386)
XLA Ops:
  0.6 39.8 %shard_map.120 = (bf16[128,1024]{1,0:T(8,128)(2,1)}, bf16[128,1024]{1,0:T(8,128)(2,1)}, f32[1,128]{1,0:T(1,128)}) custom-call(bf16[128,1024]{1,0:T(8,128)(2,1)} %value.3, bf16[1024,128]{1,0:T(8,128)(2,1)} %filt.1, bf16[128,1024]{1,0:T(8,128)(2,1)} %gate.3, bf16[128,1024]{1,0:T(8,128)(2,1)} %cot.3, f32[1,1024]{1,0:T(1,128)} %bitcast.2, s32[8]{0:T(128)} %owner.1, ...), custom_call_target="tpu_custom_call" | custom-call | tf_op jit(solution)/shard_map/pallas_call | solution.py:411
  40.4 2.2 %shard_map.121 = (bf16[128,1024]{1,0:T(8,128)(2,1)}, bf16[128,1024]{1,0:T(8,128)(2,1)}, bf16[128,1024]{1,0:T(8,128)(2,1)}, f32[1,128]{1,0:T(1,128)}) custom-call(bf16[128,1024]{1,0:T(8,128)(2,1)} %get-tuple-element.11.conv, bf16[128,1024]{1,0:T(8,128)(2,1)} %get-tuple-element.12.back, bf16[128,1024]{1,0:T(8,128)(2,1)} %value.3, bf16[128,1024]{1,0:T(8,128)(2,1)} %gate.3, ...), custom_call_target="tpu_custom_call" | custom-call | tf_op jit(solution)/shard_map/pallas_call | solution.py:476
